TPU v7x, 128 devices: a whole 4x4x4 slice. The times are simulated.
128 devices in a mesh: row: 4 (over x_hi, core), sector: 32 (over x_lo, y, z).
Axes of the slice: x: 4 (x_hi: 2, x_lo: 2; x = x_hi * 2 + x_lo), y: 4, z: 4, core: 2. Of those that a mesh axis runs over, the one named last changes fastest.
Arguments:
- state: float32 [6, 256, 512, 128], P(None, 'row', 'sector'), may hold values from -6 to 6
- interp_blocks: float32 [16, 16, 32], replicated, may hold values from -0.1 to 0.8
- rotor_offset: int32 [4, 3], replicated, may hold values from 0 to 511
- axial_speed: float32 [6], replicated, may hold values from 0.3 to 1.5
- row_swirl: float32 [4], P('row'), may hold values from -1.5 to 1.5
- diffusivity: float32 [6], replicated, may hold values from 0.05 to 0.3
- coupling: float32 [6, 6], replicated, may hold values from -1.5 to 1.5
Outputs:
- advanced: float32 [6, 256, 512, 128], P(None, 'row', 'sector')
All inputs are finite; a program needn't handle non-finite values.
Results may differ from a plain program's by a relative error of at most 0.0001.
Values sent between devices are 32-bit elements; how exact they have to be, the bound alone decides.
A program may use at most 128 MiB of HBM per device.

v0:
```python
import jax
import jax.numpy as jnp
from jax import lax
from jax.sharding import PartitionSpec as P

time_step = 0.4
highest = lax.Precision.HIGHEST


def shifted(value, axis, by):
    size = lax.axis_size(axis)
    return lax.ppermute(value, axis, [(i, (i + by) % size) for i in range(size)])


def from_behind(block, axis, distance):
    devices = range(lax.axis_size(axis))
    route = [(i - distance, i) for i in devices if i - distance in devices]
    return lax.ppermute(block, axis, route)


def extended(block, sides, width):
    for axis, dim in sides:
        count = lax.axis_size(axis)
        forward = [(i, i + 1) for i in range(count - 1)]
        forward.append((count - 1, 0))
        backward = [(target, source) for source, target in forward]
        low = lax.ppermute(
            lax.slice_in_dim(block, block.shape[dim] - width, None, axis=dim), axis, forward
        )
        high = lax.ppermute(lax.slice_in_dim(block, 0, width, axis=dim), axis, backward)
        block = jnp.concatenate([low, block, high], axis=dim)
    return block


def residual_of(center, axial_pad, cycle_pad, axial_speed, swirl_speed, diffusivity, coupling):
    d_axial = (
        -axial_pad[:, 4:] + 8.0 * axial_pad[:, 3:-1] - 8.0 * axial_pad[:, 1:-3] + axial_pad[:, :-4]
    ) / 12.0
    l_axial = (
        -axial_pad[:, 4:]
        + 16.0 * axial_pad[:, 3:-1]
        - 30.0 * center
        + 16.0 * axial_pad[:, 1:-3]
        - axial_pad[:, :-4]
    ) / 12.0
    d_cycle = (
        -cycle_pad[:, :, 4:]
        + 8.0 * cycle_pad[:, :, 3:-1]
        - 8.0 * cycle_pad[:, :, 1:-3]
        + cycle_pad[:, :, :-4]
    ) / 12.0
    l_cycle = (
        -cycle_pad[:, :, 4:]
        + 16.0 * cycle_pad[:, :, 3:-1]
        - 30.0 * center
        + 16.0 * cycle_pad[:, :, 1:-3]
        - cycle_pad[:, :, :-4]
    ) / 12.0
    radial_pad = jnp.pad(center, ((0, 0), (0, 0), (0, 0), (1, 1)))
    l_radial = radial_pad[..., 2:] - 2.0 * center + radial_pad[..., :-2]
    mixing = jnp.einsum("fg,gatr->fatr", coupling, center, precision=highest)
    speed_col = axial_speed[:, None, None, None]
    diff_col = diffusivity[:, None, None, None]
    return (
        -speed_col * d_axial
        - swirl_speed * d_cycle
        + diff_col * (l_axial + l_cycle + l_radial)
        + mixing
    )


def on_device(state, interp_blocks, rotor_offset, axial_speed, row_swirl, diffusivity, coupling):
    axial_cells = state.shape[1]
    cycle_cells = state.shape[2]
    sector_count = lax.axis_size("sector")
    row_count = lax.axis_size("row")
    row_here = lax.axis_index("row")
    full_cycle = cycle_cells * sector_count
    swirl_speed = row_swirl[0]

    def rotate_planes(section_index, upper_planes, lower_planes):
        offset_up = rotor_offset[section_index, jnp.maximum(row_here - 1, 0)]
        offset_down = (
            full_cycle - rotor_offset[section_index, jnp.minimum(row_here, row_count - 2)]
        ) % full_cycle
        sector_shifts = (offset_up // cycle_cells, offset_down // cycle_cells)
        cell_shifts = (offset_up % cycle_cells, offset_down % cycle_cells)
        moving = (upper_planes, lower_planes)
        for bit_index in range((sector_count - 1).bit_length()):
            stepped = shifted((moving[0], moving[1]), "sector", -(1 << bit_index))
            moving = tuple(
                (
                    jnp.where(
                        sector_shifts[side_index] // (1 << bit_index) % 2 == 1,
                        stepped[side_index],
                        moving[side_index],
                    )
                    for side_index in range(2)
                )
            )
        following = shifted((moving[0], moving[1]), "sector", -1)
        paired = [
            jnp.concatenate([moving[side_index], following[side_index]], axis=2)
            for side_index in range(2)
        ]
        results = []
        for side_index in range(2):
            weights = lax.dynamic_index_in_dim(
                interp_blocks, cell_shifts[side_index], 0, keepdims=False
            )
            results.append(
                jnp.einsum("jk,fakr->fajr", weights, paired[side_index], precision=highest)
            )
        return (results[0], results[1])

    def residual(current, section_index):
        upper_planes = from_behind(current[:, axial_cells - 2 :], "row", 1)
        lower_planes = from_behind(current[:, :2], "row", -1)
        ghost_up, ghost_down = rotate_planes(section_index, upper_planes, lower_planes)
        axial_pad = jnp.concatenate([ghost_up, current, ghost_down], axis=1)
        cycle_pad = extended(current, (("sector", 2),), 2)
        return residual_of(
            current, axial_pad, cycle_pad, axial_speed, swirl_speed, diffusivity, coupling
        )

    first_rate = residual(state, 0)
    second_rate = residual(state + 0.5 * time_step * first_rate, 1)
    third_rate = residual(state + 0.5 * time_step * second_rate, 2)
    fourth_rate = residual(state + time_step * third_rate, 3)
    return state + time_step / 6.0 * (
        first_rate + 2.0 * second_rate + 2.0 * third_rate + fourth_rate
    )


def solution(mesh):
    return jax.shard_map(
        on_device,
        mesh=mesh,
        in_specs=(P(None, "row", "sector", None), P(), P(), P(), P("row"), P(), P()),
        out_specs=P(None, "row", "sector", None),
        check_vma=False,
    )
```

profile of v0, /device:TPU:4, one launch (start us, length us, event | category | flops | bytes accessed | tf_op | source)
XLA Modules:
  0.0 472.7 jit_solution(4112164210251144588)
XLA Ops:
  12.5 5.2 %collective-permute-start.14 = (f32[6,64,2,128]{3,0,2,1:T(8,128)}, f32[6,64,2,128]{3,0,2,1:T(8,128)}, u32[]{:S(2)}, u32[]{:S(2)}) collective-permute-start(f32[6,64,2,128]{3,0,2,1:T(8,128)} %get-tuple-element.17), channel_id=1, source_target_pairs={{1,0},{2,1},{3,2},{4,3},{5,4},{6,5},{7,6},{8,7},{9,8},{10,9},{11,1... | collective-permute-start | bytes 1179656 | tf_op jit(solution)/shard_map/ppermute | solution.py:30
  56.1 14.4 %collective-permute-start.13 = (f32[6,2,16,128]{3,2,1,0:T(8,128)S(1)}, f32[6,2,16,128]{3,2,1,0:T(8,128)S(1)}, u32[]{:S(2)}, u32[]{:S(2)}) collective-permute-start(f32[6,2,16,128]{3,2,1,0:T(8,128)S(1)} %broadcast_select_fusion.34), channel_id=1, source_target_pairs={{0,31},{1,0},{2,1},{3,2},{4,3},{5,4},{6,5},{7,6},{8,7},{9,8},{10,9... | collective-permute-start | bytes 294920 | tf_op jit(solution)/shard_map/ppermute | solution.py:12
  73.1 5.4 %copy_dynamic-update-slice_fusion.3 = (f32[6,66,16,128]{3,0,2,1:T(8,128)}, f32[6,66,16,128]{3,0,2,1:T(8,128)S(1)}, f32[6,64,18,128]{3,0,2,1:T(8,128)}, f32[6,64,18,128]{3,0,2,1:T(8,128)S(1)}) fusion(f32[6,64,16,128]{3,2,1,0:T(8,128)S(1)} %copy-done.1, f32[6,66,16,128]{3,0,2,1:T(8,128)S(1)} %copy_dynamic-update-slice_fusion.4, ...), kind=kLoop, calls=%fused_computation.99 | loop fusion | bytes 19922944
  83.9 22.9 %multiply_add_fusion.2 = (f32[6,64,16,128]{3,0,2,1:T(8,128)}, f32[6,64,16,128]{3,0,2,1:T(8,128)}) fusion(f32[6,64,16,128]{3,2,1,0:T(8,128)S(1)} %copy-done.1, f32[6,6]{1,0:T(8,128)S(1)} %copy-done.12, f32[6,64,16,128]{3,0,2,1:T(8,128)} %copy-done.2, f32[6]{0:T(128)S(1)} %copy-done.14, f32[]{:T(128)} %bitcast.10, f32[6,64,18,128]{3,0,2,1:T(8,128)} %copy-done.3, ...), kind=kOutput, calls=%fused_computation.93 | convolution fusion | flops 87293952 | bytes 40899588 | tf_op jit(solution)/shard_map/fg,gatr->fatr/dot_general | solution.py:61
  114.1 5.1 %collective-permute-start.16 = (f32[6,2,16,128]{3,0,2,1:T(8,128)S(1)}, f32[6,2,16,128]{3,0,2,1:T(8,128)S(1)}, u32[]{:S(2)}, u32[]{:S(2)}) collective-permute-start(f32[6,2,16,128]{3,0,2,1:T(8,128)S(1)} %get-tuple-element.13), channel_id=1, source_target_pairs={{32,0},{64,32},{96,64},{33,1},{65,33},{97,65},{34,2},{66,34},{98,6... | collective-permute-start | bytes 294920 | tf_op jit(solution)/shard_map/ppermute | solution.py:18
  119.3 6.7 %collective-permute-start.24 = (f32[6,2,16,128]{3,0,2,1:T(8,128)S(1)}, f32[6,2,16,128]{3,0,2,1:T(8,128)S(1)}, u32[]{:S(2)}, u32[]{:S(2)}) collective-permute-start(f32[6,2,16,128]{3,0,2,1:T(8,128)S(1)} %collective-permute-done.23), channel_id=1, source_target_pairs={{0,31},{1,0},{2,1},{3,2},{4,3},{5,4},{6,5},{7,6},{8,7},{9,8},{10,9... | collective-permute-start | bytes 294920 | tf_op jit(solution)/shard_map/ppermute | solution.py:12
  127.4 6.2 %collective-permute-start.30 = (f32[6,64,2,128]{3,0,2,1:T(8,128)S(1)}, f32[6,64,2,128]{3,0,2,1:T(8,128)S(1)}, u32[]{:S(2)}, u32[]{:S(2)}) collective-permute-start(f32[6,64,2,128]{3,0,2,1:T(8,128)S(1)} %get-tuple-element.15), channel_id=1, source_target_pairs={{1,0},{2,1},{3,2},{4,3},{5,4},{6,5},{7,6},{8,7},{9,8},{10,9},{11,1... | collective-permute-start | bytes 1179656 | tf_op jit(solution)/shard_map/ppermute | solution.py:30
  133.7 17.7 %collective-permute-done.17 = f32[6,2,16,128]{3,0,2,1:T(8,128)S(1)} collective-permute-done((f32[6,2,16,128]{3,0,2,1:T(8,128)S(1)}, f32[6,2,16,128]{3,0,2,1:T(8,128)S(1)}, u32[]{:S(2)}, u32[]{:S(2)}) %collective-permute-start.17) | collective-permute-done | bytes 98336 | tf_op jit(solution)/shard_map/ppermute | solution.py:12
  172.0 13.5 %collective-permute-start.29 = (f32[6,2,16,128]{3,0,2,1:T(8,128)S(1)}, f32[6,2,16,128]{3,0,2,1:T(8,128)S(1)}, u32[]{:S(2)}, u32[]{:S(2)}) collective-permute-start(f32[6,2,16,128]{3,0,2,1:T(8,128)S(1)} %broadcast_select_fusion.24), channel_id=1, source_target_pairs={{0,31},{1,0},{2,1},{3,2},{4,3},{5,4},{6,5},{7,6},{8,7},{9,8},{10,9... | collective-permute-start | bytes 294920 | tf_op jit(solution)/shard_map/ppermute | solution.py:12
  195.2 31.4 %multiply_add_fusion.1 = (f32[6,64,16,128]{3,0,2,1:T(8,128)}, f32[6,64,16,128]{3,0,2,1:T(8,128)}) fusion(f32[6,64,16,128]{3,2,1,0:T(8,128)S(1)} %copy-done.1, f32[6,64,16,128]{3,0,2,1:T(8,128)} %get-tuple-element.33, f32[6,6]{1,0:T(8,128)S(1)} %copy-done.12, f32[6]{0:T(128)S(1)} %copy-done.14, f32[]{:T(128)} %bitcast.10, f32[6,64,2,128]{3,0,2,1:T(8,128)} %copy-done.7, ...), kind=kOutput, calls=%fused_computation.92 | convolution fusion | flops 93585408 | bytes 19071680 | tf_op jit(solution)/shard_map/fg,gatr->fatr/dot_general | solution.py:61
  233.5 5.1 %collective-permute-start.32 = (f32[6,2,16,128]{3,0,2,1:T(8,128)S(1)}, f32[6,2,16,128]{3,0,2,1:T(8,128)S(1)}, u32[]{:S(2)}, u32[]{:S(2)}) collective-permute-start(f32[6,2,16,128]{3,0,2,1:T(8,128)S(1)} %get-tuple-element.9), channel_id=1, source_target_pairs={{32,0},{64,32},{96,64},{33,1},{65,33},{97,65},{34,2},{66,34},{98,6... | collective-permute-start | bytes 294920 | tf_op jit(solution)/shard_map/ppermute | solution.py:18
  238.6 6.7 %collective-permute-start.40 = (f32[6,2,16,128]{3,0,2,1:T(8,128)S(1)}, f32[6,2,16,128]{3,0,2,1:T(8,128)S(1)}, u32[]{:S(2)}, u32[]{:S(2)}) collective-permute-start(f32[6,2,16,128]{3,0,2,1:T(8,128)S(1)} %collective-permute-done.39), channel_id=1, source_target_pairs={{0,31},{1,0},{2,1},{3,2},{4,3},{5,4},{6,5},{7,6},{8,7},{9,8},{10,9... | collective-permute-start | bytes 294920 | tf_op jit(solution)/shard_map/ppermute | solution.py:12
  246.7 6.2 %collective-permute-start.46 = (f32[6,64,2,128]{3,0,2,1:T(8,128)S(1)}, f32[6,64,2,128]{3,0,2,1:T(8,128)S(1)}, u32[]{:S(2)}, u32[]{:S(2)}) collective-permute-start(f32[6,64,2,128]{3,0,2,1:T(8,128)S(1)} %get-tuple-element.11), channel_id=1, source_target_pairs={{1,0},{2,1},{3,2},{4,3},{5,4},{6,5},{7,6},{8,7},{9,8},{10,9},{11,1... | collective-permute-start | bytes 1179656 | tf_op jit(solution)/shard_map/ppermute | solution.py:30
  253.1 17.7 %collective-permute-done.33 = f32[6,2,16,128]{3,0,2,1:T(8,128)S(1)} collective-permute-done((f32[6,2,16,128]{3,0,2,1:T(8,128)S(1)}, f32[6,2,16,128]{3,0,2,1:T(8,128)S(1)}, u32[]{:S(2)}, u32[]{:S(2)}) %collective-permute-start.33) | collective-permute-done | bytes 98336 | tf_op jit(solution)/shard_map/ppermute | solution.py:12
  290.9 14.1 %collective-permute-start.45 = (f32[6,2,16,128]{3,0,2,1:T(8,128)S(1)}, f32[6,2,16,128]{3,0,2,1:T(8,128)S(1)}, u32[]{:S(2)}, u32[]{:S(2)}) collective-permute-start(f32[6,2,16,128]{3,0,2,1:T(8,128)S(1)} %broadcast_select_fusion.14), channel_id=1, source_target_pairs={{0,31},{1,0},{2,1},{3,2},{4,3},{5,4},{6,5},{7,6},{8,7},{9,8},{10,9... | collective-permute-start | bytes 294920 | tf_op jit(solution)/shard_map/ppermute | solution.py:12
  304.9 5.1 %collective-permute-start.38 = (f32[6,2,16,128]{3,0,2,1:T(8,128)S(1)}, f32[6,2,16,128]{3,0,2,1:T(8,128)S(1)}, u32[]{:S(2)}, u32[]{:S(2)}) collective-permute-start(f32[6,2,16,128]{3,0,2,1:T(8,128)S(1)} %broadcast_select_fusion.19), channel_id=1, source_target_pairs={{0,31},{1,0},{2,1},{3,2},{4,3},{5,4},{6,5},{7,6},{8,7},{9,8},{10,9... | collective-permute-start | bytes 294920 | tf_op jit(solution)/shard_map/ppermute | solution.py:12
  314.5 31.3 %multiply_add_fusion = (f32[6,64,16,128]{3,0,2,1:T(8,128)}, f32[6,64,16,128]{3,0,2,1:T(8,128)}) fusion(f32[6,64,16,128]{3,2,1,0:T(8,128)S(1)} %copy-done.1, f32[6,64,16,128]{3,0,2,1:T(8,128)} %get-tuple-element.35, f32[6,6]{1,0:T(8,128)S(1)} %copy-done.12, f32[6]{0:T(128)S(1)} %copy-done.14, f32[]{:T(128)} %bitcast.10, f32[6,64,2,128]{3,0,2,1:T(8,128)} %copy-done.9, ...), kind=kOutput, calls=%fused_computation.91 | convolution fusion | flops 93585408 | bytes 19071680 | tf_op jit(solution)/shard_map/fg,gatr->fatr/dot_general | solution.py:61
  352.6 5.1 %collective-permute-start.48 = (f32[6,2,16,128]{3,0,2,1:T(8,128)S(1)}, f32[6,2,16,128]{3,0,2,1:T(8,128)S(1)}, u32[]{:S(2)}, u32[]{:S(2)}) collective-permute-start(f32[6,2,16,128]{3,0,2,1:T(8,128)S(1)} %get-tuple-element.5), channel_id=1, source_target_pairs={{32,0},{64,32},{96,64},{33,1},{65,33},{97,65},{34,2},{66,34},{98,6... | collective-permute-start | bytes 294920 | tf_op jit(solution)/shard_map/ppermute | solution.py:18
  357.7 6.7 %collective-permute-start.56 = (f32[6,2,16,128]{3,0,2,1:T(8,128)S(1)}, f32[6,2,16,128]{3,0,2,1:T(8,128)S(1)}, u32[]{:S(2)}, u32[]{:S(2)}) collective-permute-start(f32[6,2,16,128]{3,0,2,1:T(8,128)S(1)} %collective-permute-done.55), channel_id=1, source_target_pairs={{0,31},{1,0},{2,1},{3,2},{4,3},{5,4},{6,5},{7,6},{8,7},{9,8},{10,9... | collective-permute-start | bytes 294920 | tf_op jit(solution)/shard_map/ppermute | solution.py:12
  365.8 6.2 %collective-permute-start.62 = (f32[6,64,2,128]{3,0,2,1:T(8,128)S(1)}, f32[6,64,2,128]{3,0,2,1:T(8,128)S(1)}, u32[]{:S(2)}, u32[]{:S(2)}) collective-permute-start(f32[6,64,2,128]{3,0,2,1:T(8,128)S(1)} %get-tuple-element.7), channel_id=1, source_target_pairs={{1,0},{2,1},{3,2},{4,3},{5,4},{6,5},{7,6},{8,7},{9,8},{10,9},{11,1... | collective-permute-start | bytes 1179656 | tf_op jit(solution)/shard_map/ppermute | solution.py:30
  372.2 17.7 %collective-permute-done.49 = f32[6,2,16,128]{3,0,2,1:T(8,128)S(1)} collective-permute-done((f32[6,2,16,128]{3,0,2,1:T(8,128)S(1)}, f32[6,2,16,128]{3,0,2,1:T(8,128)S(1)}, u32[]{:S(2)}, u32[]{:S(2)}) %collective-permute-start.49) | collective-permute-done | bytes 98336 | tf_op jit(solution)/shard_map/ppermute | solution.py:12
  410.0 14.1 %collective-permute-start.61 = (f32[6,2,16,128]{3,0,2,1:T(8,128)S(1)}, f32[6,2,16,128]{3,0,2,1:T(8,128)S(1)}, u32[]{:S(2)}, u32[]{:S(2)}) collective-permute-start(f32[6,2,16,128]{3,0,2,1:T(8,128)S(1)} %broadcast_select_fusion.4), channel_id=1, source_target_pairs={{0,31},{1,0},{2,1},{3,2},{4,3},{5,4},{6,5},{7,6},{8,7},{9,8},{10,9... | collective-permute-start | bytes 294920 | tf_op jit(solution)/shard_map/ppermute | solution.py:12
  424.0 5.2 %collective-permute-start.54 = (f32[6,2,16,128]{3,0,2,1:T(8,128)S(1)}, f32[6,2,16,128]{3,0,2,1:T(8,128)S(1)}, u32[]{:S(2)}, u32[]{:S(2)}) collective-permute-start(f32[6,2,16,128]{3,0,2,1:T(8,128)S(1)} %broadcast_select_fusion.9), channel_id=1, source_target_pairs={{0,31},{1,0},{2,1},{3,2},{4,3},{5,4},{6,5},{7,6},{8,7},{9,8},{10,9... | collective-permute-start | bytes 294920 | tf_op jit(solution)/shard_map/ppermute | solution.py:12
  433.7 34.3 %fusion.44 = f32[6,64,16,128]{3,0,2,1:T(8,128)} fusion(f32[6,64,16,128]{3,0,2,1:T(8,128)} %get-tuple-element.37, f32[6,64,2,128]{3,0,2,1:T(8,128)} %copy-done.6, f32[6,64,2,128]{3,0,2,1:T(8,128)} %copy-done.8, f32[6,2,16,128]{3,0,2,1:T(8,128)S(1)} %bitcast.111, f32[6,2,16,128]{3,0,2,1:T(8,128)S(1)} %bitcast.113, f32[6,64,16,128]{3,0,2,1:T(8,128)} %get-tuple-element.38, ...), kind=kOutput, calls=%fused_computation.76 | convolution fusion | flops 97517568 | bytes 28508864 | tf_op jit(solution)/shard_map/fg,gatr->fatr/dot_general | solution.py:61
  (214 shorter events, 153.5 us)
Async XLA Ops:
  1.6 20.3 %collective-permute-start.7 = (f32[6,2,16,128]{3,2,1,0:T(8,128)S(1)}, f32[6,2,16,128]{3,2,1,0:T(8,128)S(1)}, u32[]{:S(2)}, u32[]{:S(2)}) collective-permute-start(f32[6,2,16,128]{3,2,1,0:T(8,128)S(1)} %get-tuple-element.20), channel_id=1, source_target_pairs={{0,32},{32,64},{64,96},{1,33},{33,65},{65,97},{2,34},{34,66},{66,9... | collective-permute-start | bytes 294920 | tf_op jit(solution)/shard_map/ppermute | solution.py:18
  10.5 38.9 %collective-permute-start.15 = (f32[6,64,2,128]{3,0,2,1:T(8,128)}, f32[6,64,2,128]{3,0,2,1:T(8,128)}, u32[]{:S(2)}, u32[]{:S(2)}) collective-permute-start(f32[6,64,2,128]{3,0,2,1:T(8,128)} %get-tuple-element.18), channel_id=1, source_target_pairs={{0,1},{1,2},{2,3},{3,4},{4,5},{5,6},{6,7},{7,8},{8,9},{9,10},{10,1... | collective-permute-start | bytes 1179656 | tf_op jit(solution)/shard_map/ppermute | solution.py:27
  12.5 68.2 %collective-permute-start.14 = (f32[6,64,2,128]{3,0,2,1:T(8,128)}, f32[6,64,2,128]{3,0,2,1:T(8,128)}, u32[]{:S(2)}, u32[]{:S(2)}) collective-permute-start(f32[6,64,2,128]{3,0,2,1:T(8,128)} %get-tuple-element.17), channel_id=1, source_target_pairs={{1,0},{2,1},{3,2},{4,3},{5,4},{6,5},{7,6},{8,7},{9,8},{10,9},{11,1... | collective-permute-start | bytes 1179656 | tf_op jit(solution)/shard_map/ppermute | solution.py:30
  56.1 16.6 %collective-permute-start.13 = (f32[6,2,16,128]{3,2,1,0:T(8,128)S(1)}, f32[6,2,16,128]{3,2,1,0:T(8,128)S(1)}, u32[]{:S(2)}, u32[]{:S(2)}) collective-permute-start(f32[6,2,16,128]{3,2,1,0:T(8,128)S(1)} %broadcast_select_fusion.34), channel_id=1, source_target_pairs={{0,31},{1,0},{2,1},{3,2},{4,3},{5,4},{6,5},{7,6},{8,7},{9,8},{10,9... | collective-permute-start | bytes 294920 | tf_op jit(solution)/shard_map/ppermute | solution.py:12
  114.1 19.5 %collective-permute-start.16 = (f32[6,2,16,128]{3,0,2,1:T(8,128)S(1)}, f32[6,2,16,128]{3,0,2,1:T(8,128)S(1)}, u32[]{:S(2)}, u32[]{:S(2)}) collective-permute-start(f32[6,2,16,128]{3,0,2,1:T(8,128)S(1)} %get-tuple-element.13), channel_id=1, source_target_pairs={{32,0},{64,32},{96,64},{33,1},{65,33},{97,65},{34,2},{66,34},{98,6... | collective-permute-start | bytes 294920 | tf_op jit(solution)/shard_map/ppermute | solution.py:18
  127.3 66.3 %collective-permute-start.31 = (f32[6,64,2,128]{3,0,2,1:T(8,128)S(1)}, f32[6,64,2,128]{3,0,2,1:T(8,128)S(1)}, u32[]{:S(2)}, u32[]{:S(2)}) collective-permute-start(f32[6,64,2,128]{3,0,2,1:T(8,128)S(1)} %get-tuple-element.16), channel_id=1, source_target_pairs={{0,1},{1,2},{2,3},{3,4},{4,5},{5,6},{6,7},{7,8},{8,9},{9,10},{10,1... | collective-permute-start | bytes 1179656 | tf_op jit(solution)/shard_map/ppermute | solution.py:27
  127.4 66.2 %collective-permute-start.30 = (f32[6,64,2,128]{3,0,2,1:T(8,128)S(1)}, f32[6,64,2,128]{3,0,2,1:T(8,128)S(1)}, u32[]{:S(2)}, u32[]{:S(2)}) collective-permute-start(f32[6,64,2,128]{3,0,2,1:T(8,128)S(1)} %get-tuple-element.15), channel_id=1, source_target_pairs={{1,0},{2,1},{3,2},{4,3},{5,4},{6,5},{7,6},{8,7},{9,8},{10,9},{11,1... | collective-permute-start | bytes 1179656 | tf_op jit(solution)/shard_map/ppermute | solution.py:30
  133.6 17.8 %collective-permute-start.17 = (f32[6,2,16,128]{3,0,2,1:T(8,128)S(1)}, f32[6,2,16,128]{3,0,2,1:T(8,128)S(1)}, u32[]{:S(2)}, u32[]{:S(2)}) collective-permute-start(f32[6,2,16,128]{3,0,2,1:T(8,128)S(1)} %collective-permute-done.16), channel_id=1, source_target_pairs={{0,31},{1,0},{2,1},{3,2},{4,3},{5,4},{6,5},{7,6},{8,7},{9,8},{10,9... | collective-permute-start | bytes 294920 | tf_op jit(solution)/shard_map/ppermute | solution.py:12
  133.6 20.6 %collective-permute-start.25 = (f32[6,2,16,128]{3,0,2,1:T(8,128)S(1)}, f32[6,2,16,128]{3,0,2,1:T(8,128)S(1)}, u32[]{:S(2)}, u32[]{:S(2)}) collective-permute-start(f32[6,2,16,128]{3,0,2,1:T(8,128)S(1)} %broadcast_select_fusion.20), channel_id=1, source_target_pairs={{0,30},{1,31},{2,0},{3,1},{4,2},{5,3},{6,4},{7,5},{8,6},{9,7},{10,... | collective-permute-start | bytes 294920 | tf_op jit(solution)/shard_map/ppermute | solution.py:12
  172.0 18.6 %collective-permute-start.29 = (f32[6,2,16,128]{3,0,2,1:T(8,128)S(1)}, f32[6,2,16,128]{3,0,2,1:T(8,128)S(1)}, u32[]{:S(2)}, u32[]{:S(2)}) collective-permute-start(f32[6,2,16,128]{3,0,2,1:T(8,128)S(1)} %broadcast_select_fusion.24), channel_id=1, source_target_pairs={{0,31},{1,0},{2,1},{3,2},{4,3},{5,4},{6,5},{7,6},{8,7},{9,8},{10,9... | collective-permute-start | bytes 294920 | tf_op jit(solution)/shard_map/ppermute | solution.py:12
  233.5 19.5 %collective-permute-start.32 = (f32[6,2,16,128]{3,0,2,1:T(8,128)S(1)}, f32[6,2,16,128]{3,0,2,1:T(8,128)S(1)}, u32[]{:S(2)}, u32[]{:S(2)}) collective-permute-start(f32[6,2,16,128]{3,0,2,1:T(8,128)S(1)} %get-tuple-element.9), channel_id=1, source_target_pairs={{32,0},{64,32},{96,64},{33,1},{65,33},{97,65},{34,2},{66,34},{98,6... | collective-permute-start | bytes 294920 | tf_op jit(solution)/shard_map/ppermute | solution.py:18
  246.6 66.3 %collective-permute-start.47 = (f32[6,64,2,128]{3,0,2,1:T(8,128)S(1)}, f32[6,64,2,128]{3,0,2,1:T(8,128)S(1)}, u32[]{:S(2)}, u32[]{:S(2)}) collective-permute-start(f32[6,64,2,128]{3,0,2,1:T(8,128)S(1)} %get-tuple-element.12), channel_id=1, source_target_pairs={{0,1},{1,2},{2,3},{3,4},{4,5},{5,6},{6,7},{7,8},{8,9},{9,10},{10,1... | collective-permute-start | bytes 1179656 | tf_op jit(solution)/shard_map/ppermute | solution.py:27
  246.7 66.2 %collective-permute-start.46 = (f32[6,64,2,128]{3,0,2,1:T(8,128)S(1)}, f32[6,64,2,128]{3,0,2,1:T(8,128)S(1)}, u32[]{:S(2)}, u32[]{:S(2)}) collective-permute-start(f32[6,64,2,128]{3,0,2,1:T(8,128)S(1)} %get-tuple-element.11), channel_id=1, source_target_pairs={{1,0},{2,1},{3,2},{4,3},{5,4},{6,5},{7,6},{8,7},{9,8},{10,9},{11,1... | collective-permute-start | bytes 1179656 | tf_op jit(solution)/shard_map/ppermute | solution.py:30
  253.0 17.8 %collective-permute-start.33 = (f32[6,2,16,128]{3,0,2,1:T(8,128)S(1)}, f32[6,2,16,128]{3,0,2,1:T(8,128)S(1)}, u32[]{:S(2)}, u32[]{:S(2)}) collective-permute-start(f32[6,2,16,128]{3,0,2,1:T(8,128)S(1)} %collective-permute-done.32), channel_id=1, source_target_pairs={{0,31},{1,0},{2,1},{3,2},{4,3},{5,4},{6,5},{7,6},{8,7},{9,8},{10,9... | collective-permute-start | bytes 294920 | tf_op jit(solution)/shard_map/ppermute | solution.py:12
  253.0 20.6 %collective-permute-start.41 = (f32[6,2,16,128]{3,0,2,1:T(8,128)S(1)}, f32[6,2,16,128]{3,0,2,1:T(8,128)S(1)}, u32[]{:S(2)}, u32[]{:S(2)}) collective-permute-start(f32[6,2,16,128]{3,0,2,1:T(8,128)S(1)} %broadcast_select_fusion.10), channel_id=1, source_target_pairs={{0,30},{1,31},{2,0},{3,1},{4,2},{5,3},{6,4},{7,5},{8,6},{9,7},{10,... | collective-permute-start | bytes 294920 | tf_op jit(solution)/shard_map/ppermute | solution.py:12
  289.0 15.9 %collective-permute-start.37 = (f32[6,2,16,128]{3,0,2,1:T(8,128)S(1)}, f32[6,2,16,128]{3,0,2,1:T(8,128)S(1)}, u32[]{:S(2)}, u32[]{:S(2)}) collective-permute-start(f32[6,2,16,128]{3,0,2,1:T(8,128)S(1)} %broadcast_select_fusion.18), channel_id=1, source_target_pairs={{0,16},{1,17},{2,18},{3,19},{4,20},{5,21},{6,22},{7,23},{8,24},{9,... | collective-permute-start | bytes 294920 | tf_op jit(solution)/shard_map/ppermute | solution.py:12
  290.9 19.2 %collective-permute-start.45 = (f32[6,2,16,128]{3,0,2,1:T(8,128)S(1)}, f32[6,2,16,128]{3,0,2,1:T(8,128)S(1)}, u32[]{:S(2)}, u32[]{:S(2)}) collective-permute-start(f32[6,2,16,128]{3,0,2,1:T(8,128)S(1)} %broadcast_select_fusion.14), channel_id=1, source_target_pairs={{0,31},{1,0},{2,1},{3,2},{4,3},{5,4},{6,5},{7,6},{8,7},{9,8},{10,9... | collective-permute-start | bytes 294920 | tf_op jit(solution)/shard_map/ppermute | solution.py:12
  352.6 19.5 %collective-permute-start.48 = (f32[6,2,16,128]{3,0,2,1:T(8,128)S(1)}, f32[6,2,16,128]{3,0,2,1:T(8,128)S(1)}, u32[]{:S(2)}, u32[]{:S(2)}) collective-permute-start(f32[6,2,16,128]{3,0,2,1:T(8,128)S(1)} %get-tuple-element.5), channel_id=1, source_target_pairs={{32,0},{64,32},{96,64},{33,1},{65,33},{97,65},{34,2},{66,34},{98,6... | collective-permute-start | bytes 294920 | tf_op jit(solution)/shard_map/ppermute | solution.py:18
  365.7 66.3 %collective-permute-start.63 = (f32[6,64,2,128]{3,0,2,1:T(8,128)S(1)}, f32[6,64,2,128]{3,0,2,1:T(8,128)S(1)}, u32[]{:S(2)}, u32[]{:S(2)}) collective-permute-start(f32[6,64,2,128]{3,0,2,1:T(8,128)S(1)} %get-tuple-element.8), channel_id=1, source_target_pairs={{0,1},{1,2},{2,3},{3,4},{4,5},{5,6},{6,7},{7,8},{8,9},{9,10},{10,1... | collective-permute-start | bytes 1179656 | tf_op jit(solution)/shard_map/ppermute | solution.py:27
  365.8 66.3 %collective-permute-start.62 = (f32[6,64,2,128]{3,0,2,1:T(8,128)S(1)}, f32[6,64,2,128]{3,0,2,1:T(8,128)S(1)}, u32[]{:S(2)}, u32[]{:S(2)}) collective-permute-start(f32[6,64,2,128]{3,0,2,1:T(8,128)S(1)} %get-tuple-element.7), channel_id=1, source_target_pairs={{1,0},{2,1},{3,2},{4,3},{5,4},{6,5},{7,6},{8,7},{9,8},{10,9},{11,1... | collective-permute-start | bytes 1179656 | tf_op jit(solution)/shard_map/ppermute | solution.py:30
  372.1 17.8 %collective-permute-start.49 = (f32[6,2,16,128]{3,0,2,1:T(8,128)S(1)}, f32[6,2,16,128]{3,0,2,1:T(8,128)S(1)}, u32[]{:S(2)}, u32[]{:S(2)}) collective-permute-start(f32[6,2,16,128]{3,0,2,1:T(8,128)S(1)} %collective-permute-done.48), channel_id=1, source_target_pairs={{0,31},{1,0},{2,1},{3,2},{4,3},{5,4},{6,5},{7,6},{8,7},{9,8},{10,9... | collective-permute-start | bytes 294920 | tf_op jit(solution)/shard_map/ppermute | solution.py:12
  372.1 20.6 %collective-permute-start.57 = (f32[6,2,16,128]{3,0,2,1:T(8,128)S(1)}, f32[6,2,16,128]{3,0,2,1:T(8,128)S(1)}, u32[]{:S(2)}, u32[]{:S(2)}) collective-permute-start(f32[6,2,16,128]{3,0,2,1:T(8,128)S(1)} %broadcast_select_fusion), channel_id=1, source_target_pairs={{0,30},{1,31},{2,0},{3,1},{4,2},{5,3},{6,4},{7,5},{8,6},{9,7},{10,... | collective-permute-start | bytes 294920 | tf_op jit(solution)/shard_map/ppermute | solution.py:12
  408.1 15.9 %collective-permute-start.53 = (f32[6,2,16,128]{3,0,2,1:T(8,128)S(1)}, f32[6,2,16,128]{3,0,2,1:T(8,128)S(1)}, u32[]{:S(2)}, u32[]{:S(2)}) collective-permute-start(f32[6,2,16,128]{3,0,2,1:T(8,128)S(1)} %broadcast_select_fusion.8), channel_id=1, source_target_pairs={{0,16},{1,17},{2,18},{3,19},{4,20},{5,21},{6,22},{7,23},{8,24},{9,... | collective-permute-start | bytes 294920 | tf_op jit(solution)/shard_map/ppermute | solution.py:12
  410.0 19.2 %collective-permute-start.61 = (f32[6,2,16,128]{3,0,2,1:T(8,128)S(1)}, f32[6,2,16,128]{3,0,2,1:T(8,128)S(1)}, u32[]{:S(2)}, u32[]{:S(2)}) collective-permute-start(f32[6,2,16,128]{3,0,2,1:T(8,128)S(1)} %broadcast_select_fusion.4), channel_id=1, source_target_pairs={{0,31},{1,0},{2,1},{3,2},{4,3},{5,4},{6,5},{7,6},{8,7},{9,8},{10,9... | collective-permute-start | bytes 294920 | tf_op jit(solution)/shard_map/ppermute | solution.py:12
  (55 other events, 529.6 us)
where the time goes:
time: 478 us; the launch traced here: 473 us
  starting transfers between devices  168 us (35%)
  waiting for transfers between devices  127 us (27%)
  matrix products  122 us (26%)
  local copies, waits for them, and re-layouts  39.2 us (8%)
  between operations  15.1 us (3%)
    ppermute x48, waiting for transfers between devices, shifted(): lax.ppermute(value, axis, [(i, (i + by) % size) for i in range(size)])  124 us
    dot_general x4, matrix products, residual_of(): mixing = jnp.einsum('fg,gatr->fatr', coupling, center, precision=highest)  120 us
    ppermute x48, starting transfers between devices, shifted(): lax.ppermute(value, axis, [(i, (i + by) % size) for i in range(size)])  114 us
    ppermute x8, starting transfers between devices, from_behind(): return lax.ppermute(block, axis, route)  27.5 us
    ppermute x4, starting transfers between devices, extended(): lax.ppermute(lax.slice_in_dim(block, 0, width, axis=dim), axis, backward)  23.9 us
    unnamed x34, local copies, waits for them, and re-layouts  19.4 us
  transfers between devices with their start and end apart: 64, of which 36 were waited for; matrix products, arithmetic and copies ran while one was open for 4% of the time, Pallas kernels for 0%

commit v1 on v0

v1 whole, which is shorter than its diff:
```python
import functools

import jax
import jax.numpy as jnp
from jax import lax
from jax.experimental import pallas as pl
from jax.experimental.pallas import tpu as pltpu
from jax.sharding import PartitionSpec as P

MESH = pl.DeviceIdType.MESH
H = 0.4
F = 6
CA = 64
CT = 16
CR = 128
G = 4
LO = 8
GROUPS = ((2, 22), (22, 42), (42, 62))
CHUNKS = GROUPS + ((0, 2), (62, 64))
PIECE = (F, 2, CT, CR)


def kernel(
    state, weights, offset, speed, swirl, diffusivity, coupling, out, q, *rest
):
    held = [[rest[(g * 2 + s) * 5 : (g * 2 + s) * 5 + 5] for s in range(2)] for g in range(G)]
    load_sem, halo_send, halo_recv, one_send, one_recv, two_send, two_recv, three_send, three_recv = rest[40:]
    row = lax.axis_index("row")
    sector = lax.axis_index("sector")
    x = sector // 16
    y = (sector // 4) % 4
    z = sector % 4
    after = (sector + 1) % 32
    before = (sector + 31) % 32
    flipped = (sector + 16) % 32

    def active(side):
        return row >= 1 if side == 0 else row <= 2

    def sends(side):
        return row <= 2 if side == 0 else row >= 1

    def load(i):
        a, b = CHUNKS[i]
        return pltpu.make_async_copy(
            state.at[:, a:b], q.at[0, :, a + 2 : b + 2, LO : LO + CT, :], load_sem.at[i]
        )

    def halo(g, i, up):
        a, b = CHUNKS[i]
        source, target = (LO + CT - 2, LO - 2) if up else (LO, LO + CT)
        return pltpu.make_async_remote_copy(
            src_ref=q.at[g, :, a + 2 : b + 2, source : source + 2, :],
            dst_ref=q.at[g, :, a + 2 : b + 2, target : target + 2, :],
            send_sem=halo_send.at[g, i, up],
            recv_sem=halo_recv.at[g, i, up],
            device_id=(row, after if up else before),
            device_id_type=MESH,
        )

    def one(g, side, flip, slot):
        a = CA if side == 0 else 2
        return pltpu.make_async_remote_copy(
            src_ref=q.at[g, :, a : a + 2, LO : LO + CT, :],
            dst_ref=held[g][side][0].at[slot],
            send_sem=one_send.at[g, side, flip],
            recv_sem=one_recv.at[g, side, slot],
            device_id=(row + 1 if side == 0 else row - 1, flipped if flip else sector),
            device_id_type=MESH,
        )

    def two(g, side, d):
        return pltpu.make_async_remote_copy(
            src_ref=held[g][side][1].at[d - 1],
            dst_ref=held[g][side][2].at[y],
            send_sem=two_send.at[g, side, d - 1],
            recv_sem=two_recv.at[g, side, d - 1],
            device_id=(row, x * 16 + ((y + d) % 4) * 4 + z),
            device_id_type=MESH,
        )

    def three(g, side, d):
        return pltpu.make_async_remote_copy(
            src_ref=held[g][side][3].at[d - 1],
            dst_ref=held[g][side][4].at[z],
            send_sem=three_send.at[g, side, d - 1],
            recv_sem=three_recv.at[g, side, d - 1],
            device_id=(row, x * 16 + y * 4 + (z + d) % 4),
            device_id_type=MESH,
        )

    def digits(g, side):
        if side == 0:
            o = offset[g, jnp.maximum(row - 1, 0)]
        else:
            o = (512 - offset[g, jnp.minimum(row, 2)]) & 511
        return (o >> 8) & 1, (o >> 6) & 3, (o >> 4) & 3, o & 15

    def send_one(g):
        for side in range(2):

            @pl.when(sends(side))
            def _():
                for flip in range(2):
                    one(g, side, flip, x).start()

    def send_two(g):
        for side in range(2):

            @pl.when(active(side))
            def _():
                for slot in range(2):
                    one(g, side, 0, slot).wait_recv()
                sx, sy, sz, _ = digits(g, side)
                first, staged, second, _, _ = held[g][side]
                for d in range(4):
                    target = (y + d) % 4
                    role = jnp.where(((target + sy) & 3) == y, 0, 1)
                    pick = (x + sx + ((target + sy + role) >> 2)) & 1
                    content = first[pick]
                    if d == 0:
                        second[y] = content
                    else:
                        staged[d - 1] = content
                        two(g, side, d).start()

    def send_three(g):
        for side in range(2):

            @pl.when(active(side))
            def _():
                for d in range(1, 4):
                    two(g, side, d).wait_recv()
                sx, sy, sz, _ = digits(g, side)
                _, _, second, staged, third = held[g][side]
                for d in range(4):
                    target = (z + d) % 4
                    role = jnp.where(((target + sz) & 3) == z, 0, 1)
                    pick = (y + sy + ((target + sz + role) >> 2)) & 3
                    content = second[pick]
                    if d == 0:
                        third[z] = content
                    else:
                        staged[d - 1] = content
                        three(g, side, d).start()

    def ghosts(g):
        for side in range(2):
            a = 0 if side == 0 else CA + 2

            @pl.when(active(side))
            def _():
                for d in range(1, 4):
                    three(g, side, d).wait_recv()
                _, _, sz, cell = digits(g, side)
                third = held[g][side][4]
                near = third[(z + sz) & 3]
                far = third[(z + sz + 1) & 3]
                w = weights[cell]
                block = jnp.concatenate(
                    [
                        jnp.concatenate([near[f, p], far[f, p]], axis=0)
                        for f in range(F)
                        for p in range(2)
                    ],
                    axis=1,
                )
                got = jnp.dot(
                    w, block, precision=lax.Precision.HIGHEST, preferred_element_type=jnp.float32
                )
                for f in range(F):
                    for p in range(2):
                        n = (f * 2 + p) * CR
                        q[g, f, a + p, LO : LO + CT, :] = got[:, n : n + CR]

            @pl.when(jnp.logical_not(active(side)))
            def _():
                for f in range(F):
                    for p in range(2):
                        q[g, f, a + p, LO : LO + CT, :] = jnp.zeros((CT, CR), jnp.float32)

    lane = lax.broadcasted_iota(jnp.int32, (8, CR), 1)

    def splat(value):
        return jnp.full((8, CR), value, jnp.float32)

    def advance(g, planes):
        scale = (H / 2, H / 2, H, H / 6)[g]

        def field(f, _):
            d = splat(diffusivity[f]) * scale
            s = splat(speed[f]) * scale
            w = splat(swirl[0]) * scale
            mix = [splat(coupling[f, e]) * scale for e in range(F)]
            near_d, far_d = d * (16.0 / 12.0), d * (-1.0 / 12.0)
            a_p1, a_m1 = near_d - s * (8.0 / 12.0), near_d + s * (8.0 / 12.0)
            a_p2, a_m2 = far_d + s * (1.0 / 12.0), far_d - s * (1.0 / 12.0)
            c_p1, c_m1 = near_d - w * (8.0 / 12.0), near_d + w * (8.0 / 12.0)
            c_p2, c_m2 = far_d + w * (1.0 / 12.0), far_d - w * (1.0 / 12.0)
            centre = d * -7.0
            from_left = jnp.where(lane == 0, 0.0, d)
            from_right = jnp.where(lane == CR - 1, 0.0, d)

            def plane(a):
                for half in range(2):
                    t = LO + 8 * half

                    def at(field, by_a, by_t):
                        return q[g, field, a + 2 + by_a, t + by_t : t + by_t + 8, :]

                    own = at(f, 0, 0)
                    total = centre * own
                    for e in range(F):
                        total += mix[e] * at(e, 0, 0)
                    total += from_left * pltpu.roll(own, 1, 1)
                    total += from_right * pltpu.roll(own, CR - 1, 1)
                    ring = c_p1 * at(f, 0, 1) + c_m1 * at(f, 0, -1)
                    ring += c_p2 * at(f, 0, 2) + c_m2 * at(f, 0, -2)
                    along = a_p1 * at(f, 1, 0) + a_m1 * at(f, -1, 0)
                    along += a_p2 * at(f, 2, 0) + a_m2 * at(f, -2, 0)
                    total += ring + along

                    def stage(n):
                        return q[n, f, a + 2, t : t + 8, :]

                    if g < G - 1:
                        q[g + 1, f, a + 2, t : t + 8, :] = stage(0) + total
                    else:
                        out[f, a, 8 * half : 8 * half + 8, :] = total + (
                            stage(1) + 2.0 * stage(2) + own - stage(0)
                        ) * (1.0 / 3.0)

            if isinstance(planes[0], tuple):
                for a, b in planes:
                    for n in range(a, b):
                        plane(n)
            else:

                def pair(n, _):
                    plane(planes[0] + 2 * n)
                    plane(planes[0] + 2 * n + 1)
                    return 0

                lax.fori_loop(0, (planes[1] - planes[0]) // 2, pair, 0)
            return 0

        lax.fori_loop(0, F, field, 0)

    for i in (3, 4, 0, 1, 2):
        load(i).start()
    barrier = pltpu.get_barrier_semaphore()

    def greet(r, s):
        pl.semaphore_signal(barrier, inc=1, device_id=(r, s), device_id_type=MESH)

    greet(row, after)
    greet(row, before)
    for d in range(1, 4):
        greet(row, x * 16 + ((y + d) % 4) * 4 + z)
        greet(row, x * 16 + y * 4 + (z + d) % 4)

    @pl.when(row <= 2)
    def _():
        greet(row + 1, sector)
        greet(row + 1, flipped)

    @pl.when(row >= 1)
    def _():
        greet(row - 1, sector)
        greet(row - 1, flipped)

    pl.semaphore_wait(barrier, jnp.where(row == 0, 10, jnp.where(row == 3, 10, 12)))

    load(3).wait()
    load(4).wait()
    send_one(0)
    for i in (0, 3, 4, 1, 2):
        if i < 3:
            load(i).wait()
        for up in range(2):
            halo(0, i, up).start()

    for g in range(G):

        def group(i):
            for up in range(2):
                halo(g, i, up).wait_recv()
            advance(g, CHUNKS[i])
            if g < G - 1:
                for up in range(2):
                    halo(g + 1, i, up).start()

        group(0)
        send_two(g)
        group(1)
        send_three(g)
        group(2)
        ghosts(g)
        for i in (3, 4):
            for up in range(2):
                halo(g, i, up).wait_recv()
        advance(g, (CHUNKS[3], CHUNKS[4]))
        if g < G - 1:
            send_one(g + 1)
            for i in (3, 4):
                for up in range(2):
                    halo(g + 1, i, up).start()

    for g in range(G):
        for i in range(5):
            for up in range(2):
                halo(g, i, up).wait_send()
        for side in range(2):

            @pl.when(sends(side))
            def _():
                for flip in range(2):
                    one(g, side, flip, x).wait_send()

            @pl.when(active(side))
            def _():
                for d in range(1, 4):
                    two(g, side, d).wait_send()
                    three(g, side, d).wait_send()


def on_device(state, interp_blocks, rotor_offset, axial_speed, row_swirl, diffusivity, coupling):
    smem = pl.BlockSpec(memory_space=pltpu.SMEM)
    vmem = pl.BlockSpec(memory_space=pltpu.VMEM)
    held = []
    for _ in range(2 * G):
        for n in (2, 3, 4, 3, 4):
            held.append(pltpu.VMEM((n,) + PIECE, jnp.float32))
    dma = pltpu.SemaphoreType.DMA
    return pl.pallas_call(
        kernel,
        out_shape=jax.ShapeDtypeStruct(state.shape, jnp.float32),
        in_specs=[pl.BlockSpec(memory_space=pl.ANY), vmem, smem, smem, smem, smem, smem],
        out_specs=vmem,
        scratch_shapes=[
            pltpu.VMEM((G, F, CA + 4, 32, CR), jnp.float32),
            *held,
            dma((5,)),
            dma((G, 5, 2)),
            dma((G, 5, 2)),
            dma((G, 2, 2)),
            dma((G, 2, 2)),
            dma((G, 2, 3)),
            dma((G, 2, 3)),
            dma((G, 2, 3)),
            dma((G, 2, 3)),
        ],
        compiler_params=pltpu.CompilerParams(
            collective_id=0, has_side_effects=True, vmem_limit_bytes=64 * 1024 * 1024 - 65536
        ),
    )(state, interp_blocks, rotor_offset, axial_speed, row_swirl, diffusivity, coupling)


def solution(mesh):
    return jax.shard_map(
        on_device,
        mesh=mesh,
        in_specs=(P(None, "row", "sector", None), P(), P(), P(), P("row"), P(), P()),
        out_specs=P(None, "row", "sector", None),
        check_vma=False,
    )
```

time: 478 us -> 130 us (0.27)
  the two profiles are of different devices: /device:TPU:4 before, /device:TPU:1 now
where the time goes in v1:
time: 130 us
  Pallas kernels  125 us (96%)
  local copies, waits for them, and re-layouts  3.94 us (3%)
    pallas_call x1, Pallas kernels, on_device(): pl.pallas_call(kernel, out_shape=jax.ShapeDtypeStruct(state.shape, jnp.fl...  125 us
    unnamed x1, local copies, waits for them, and re-layouts  3.94 us

profile of v1, /device:TPU:1, one launch (start us, length us, event | category | flops | bytes accessed | tf_op | source)
XLA Modules:
  0.0 129.7 jit_solution(17207993376277453814)
XLA Ops:
  0.7 125.0 %shard_map.73 = f32[6,64,16,128]{3,2,1,0:T(8,128)} custom-call(f32[6,64,16,128]{3,2,1,0:T(8,128)} %state.1, f32[16,16,32]{2,1,0:T(8,128)} %weights.1, s32[4,3]{1,0:T(4,128)} %offset.1, f32[6]{0:T(128)} %speed.1, f32[1]{0:T(128)S(6)} %copy.9.swirl, f32[6]{0:T(128)} %diffusivity.1, f32[6,6]{1,0:T(8,128)} %coupling.1), custom_call_target="tpu_custom_call" | custom-call | tf_op jit(solution)/shard_map/pallas_call | solution.py:335
  125.7 3.9 %copy.10 = f32[6,64,16,128]{3,2,1,0:T(8,128)} copy(f32[6,64,16,128]{3,2,1,0:T(8,128)} %shard_map.73) | data formatting | bytes 6291456

commit v2 on v1

v2 whole, which is shorter than its diff:
```python
import functools

import jax
import jax.numpy as jnp
from jax import lax
from jax.experimental import pallas as pl
from jax.experimental.pallas import tpu as pltpu
from jax.sharding import PartitionSpec as P

MESH = pl.DeviceIdType.MESH
H = 0.4
F = 6
CA = 64
CT = 16
CR = 128
G = 4
LO = 8
STEP = 4
UNITS = tuple((2 + 12 * i, 14 + 12 * i, 3 * j, 3 * j + 3) for i in range(5) for j in range(2))
CHUNKS = UNITS + ((0, 2, 0, 6), (62, 64, 0, 6))
LOADS = ((0, 2), (62, 64)) + tuple((2 + 12 * i, 14 + 12 * i) for i in range(5))
N = len(UNITS)
ORDER = "CC2HC2HC2HC3HCHC3HCH3CHC4H4H4"
PIECES = 3
PF = F // PIECES
PIECE = (PF, 2, CT, CR)


def kernel(
    state, small_0, small_1, small_2, small_3, small_4, small_5, out, result, q0, q1, q2, q3, *rest
):
    q = (q0, q1, q2, q3)
    weights, offset, speed, swirl, diffusivity, coupling = rest[:6]
    rest = rest[6:]
    held = [
        [[rest[((g * 2 + s) * PIECES + p) * 5 :][:5] for p in range(PIECES)] for s in range(2)]
        for g in range(G)
    ]
    small = (
        (small_0, weights),
        (small_1, offset),
        (small_2, speed),
        (small_3, swirl),
        (small_4, diffusivity),
        (small_5, coupling),
    )
    small_sem, load_sem, store_sem, halo_send, halo_recv, turn_send, turn_recv = rest[
        2 * G * PIECES * 5 :
    ]
    row = lax.axis_index("row")
    sector = lax.axis_index("sector")
    x = sector // 16
    y = (sector // 4) % 4
    z = sector % 4
    after = (sector + 1) % 32
    before = (sector + 31) % 32
    flipped = (sector + 16) % 32

    def active(side):
        return row >= 1 if side == 0 else row <= 2

    def sends(side):
        return row <= 2 if side == 0 else row >= 1

    def load(i):
        a, b = LOADS[i]
        return pltpu.make_async_copy(
            state.at[:, a:b], q[0].at[:, a + 2 : b + 2, LO : LO + CT, :], load_sem.at[i]
        )

    def arrived(like, sem):
        pltpu.make_async_copy(like, like, sem).wait()

    def wait_halo(g, i):
        a, b, f, e = CHUNKS[i]
        arrived(q[g].at[f:e, a + 2 : b + 2, 0:4, :], halo_recv.at[g, i])

    def store(i):
        a, b, f, e = CHUNKS[i]
        return pltpu.make_async_copy(
            result.at[f:e, a:b], out.at[f:e, a:b], store_sem
        )

    def halo(g, i, up):
        a, b, f, e = CHUNKS[i]
        source, target = (LO + CT - 2, LO - 2) if up else (LO, LO + CT)
        return pltpu.make_async_remote_copy(
            src_ref=q[g].at[f:e, a + 2 : b + 2, source : source + 2, :],
            dst_ref=q[g].at[f:e, a + 2 : b + 2, target : target + 2, :],
            send_sem=halo_send.at[g],
            recv_sem=halo_recv.at[g, i],
            device_id=(row, after if up else before),
            device_id_type=MESH,
        )

    def one(g, side, p, flip, slot):
        a = CA if side == 0 else 2
        return pltpu.make_async_remote_copy(
            src_ref=q[g].at[PF * p : PF * p + PF, a : a + 2, LO : LO + CT, :],
            dst_ref=held[g][side][p][0].at[slot],
            send_sem=turn_send.at[0, side],
            recv_sem=turn_recv.at[0, g, side, p],
            device_id=(row + 1 if side == 0 else row - 1, flipped if flip else sector),
            device_id_type=MESH,
        )

    def two(g, side, p, d):
        return pltpu.make_async_remote_copy(
            src_ref=held[g][side][p][1].at[d - 1],
            dst_ref=held[g][side][p][2].at[y],
            send_sem=turn_send.at[1, side],
            recv_sem=turn_recv.at[1, g, side, p],
            device_id=(row, x * 16 + ((y + d) % 4) * 4 + z),
            device_id_type=MESH,
        )

    def three(g, side, p, d):
        return pltpu.make_async_remote_copy(
            src_ref=held[g][side][p][3].at[d - 1],
            dst_ref=held[g][side][p][4].at[z],
            send_sem=turn_send.at[2, side],
            recv_sem=turn_recv.at[2, g, side, p],
            device_id=(row, x * 16 + y * 4 + (z + d) % 4),
            device_id_type=MESH,
        )

    def digits(g, side):
        if side == 0:
            o = offset[g, jnp.maximum(row - 1, 0)]
        else:
            o = (512 - offset[g, jnp.minimum(row, 2)]) & 511
        return (o >> 8) & 1, (o >> 6) & 3, (o >> 4) & 3, o & 15

    def send_one(g, p):
        for side in range(2):

            @pl.when(sends(side))
            def _():
                for flip in range(2):
                    one(g, side, p, flip, x).start()

    def send_two(g, p):
        for side in range(2):

            @pl.when(active(side))
            def _():
                arrived(held[g][side][p][0], turn_recv.at[0, g, side, p])
                sx, sy, sz, _ = digits(g, side)
                first, staged, second, _, _ = held[g][side][p]
                for d in (1, 3, 2, 0):
                    target = (y + d) % 4
                    role = jnp.where(((target + sy) & 3) == y, 0, 1)
                    pick = (x + sx + ((target + sy + role) >> 2)) & 1
                    content = first[pick]
                    if d == 0:
                        second[y] = content
                    else:
                        staged[d - 1] = content
                        two(g, side, p, d).start()

    def send_three(g, p):
        for side in range(2):

            @pl.when(active(side))
            def _():
                arrived(held[g][side][p][1], turn_recv.at[1, g, side, p])
                sx, sy, sz, _ = digits(g, side)
                _, _, second, staged, third = held[g][side][p]
                for d in (1, 3, 2, 0):
                    target = (z + d) % 4
                    role = jnp.where(((target + sz) & 3) == z, 0, 1)
                    pick = (y + sy + ((target + sz + role) >> 2)) & 3
                    content = second[pick]
                    if d == 0:
                        third[z] = content
                    else:
                        staged[d - 1] = content
                        three(g, side, p, d).start()

    def clear():
        for side in range(2):
            a = 0 if side == 0 else CA + 2

            @pl.when(jnp.logical_not(active(side)))
            def _():
                for g in range(G):
                    q[g][:, a : a + 2, LO : LO + CT, :] = jnp.zeros((F, 2, CT, CR), jnp.float32)

    def ghosts(g, p):
        for side in range(2):
            a = 0 if side == 0 else CA + 2

            @pl.when(active(side))
            def _():
                arrived(held[g][side][p][3], turn_recv.at[2, g, side, p])
                _, _, sz, cell = digits(g, side)
                third = held[g][side][p][4]
                near = third[(z + sz) & 3]
                far = third[(z + sz + 1) & 3]
                w = weights[cell]
                block = jnp.concatenate(
                    [
                        jnp.concatenate([near[f, n], far[f, n]], axis=0)
                        for f in range(PF)
                        for n in range(2)
                    ],
                    axis=1,
                )
                got = jnp.dot(
                    w, block, precision=lax.Precision.HIGHEST, preferred_element_type=jnp.float32
                )
                for f in range(PF):
                    for n in range(2):
                        at = (f * 2 + n) * CR
                        q[g][PF * p + f, a + n, LO : LO + CT, :] = got[:, at : at + CR]

    lane = lax.broadcasted_iota(jnp.int32, (8, CR), 1)

    def splat(value):
        return jnp.full((8, CR), value, jnp.float32)

    def coefficients(g, f):
        scale = (H / 2, H / 2, H, H / 6)[g]
        d = splat(diffusivity[f]) * scale
        s = splat(speed[f]) * scale
        w = splat(swirl[0]) * scale
        mix = [
            splat(coupling[f, e]) * scale + jnp.where(splat_int(f) == e, d * -7.0, 0.0)
            for e in range(F)
        ]
        near_d, far_d = d * (16.0 / 12.0), d * (-1.0 / 12.0)
        near_s, far_s = s * (8.0 / 12.0), s * (1.0 / 12.0)
        near_w, far_w = w * (8.0 / 12.0), w * (1.0 / 12.0)
        along = (far_d - far_s, near_d + near_s, near_d - near_s, far_d + far_s)
        ring = (far_d - far_w, near_d + near_w, near_d - near_w, far_d + far_w)
        left = jnp.where(lane == 0, 0.0, d)
        right = jnp.where(lane == CR - 1, 0.0, d)
        return mix, along, ring, left, right

    def splat_int(value):
        return jnp.full((8, CR), value, jnp.int32)

    def block(g, f, coefs, a, n):
        mix, along, ring, left, right = coefs
        now = q[g]
        results = []
        for half in range(2):
            t = LO + 8 * half
            window = [now[f, a + i, t : t + 8, :] for i in range(n + 4)]
            for i in range(n):
                own = window[i + 2]
                plane = a + i + 2
                parts = [mix[e] * now[e, plane, t : t + 8, :] for e in range(F)]
                parts += [along[j] * window[i + (0, 1, 3, 4)[j]] for j in range(4)]
                parts += [
                    ring[j] * now[f, plane, t + (-2, -1, 1, 2)[j] : t + (6, 7, 9, 10)[j], :]
                    for j in range(4)
                ]
                parts += [left * pltpu.roll(own, 1, 1), right * pltpu.roll(own, CR - 1, 1)]
                if g == 0:
                    parts.append(own)
                elif g < G - 1:
                    parts.append(q[0][f, plane, t : t + 8, :])
                else:
                    two_q2 = q[2][f, plane, t : t + 8, :] * 2.0
                    three_s = q[1][f, plane, t : t + 8, :] - q[0][f, plane, t : t + 8, :]
                    parts.append(((two_q2 + three_s) + own) * (1.0 / 3.0))
                sums = [parts[0] + parts[6], parts[1] + parts[7], parts[2] + parts[8]]
                sums += [parts[3] + parts[9], parts[4] + parts[10], parts[5] + parts[11]]
                sums += [parts[12] + parts[14], parts[13] + parts[15] + parts[16]]
                total = ((sums[0] + sums[1]) + (sums[2] + sums[3])) + (
                    (sums[4] + sums[5]) + (sums[6] + sums[7])
                )
                results.append((plane, t, total))
        for plane, t, total in results:
            if g < G - 1:
                q[g + 1][f, plane, t : t + 8, :] = total
            else:
                result[f, plane - 2, t - LO : t - LO + 8, :] = total

    def interior(g, i):
        start, stop, low, high = CHUNKS[i]

        def field(f, _):
            coefs = coefficients(g, f)

            def step(n, _):
                block(g, f, coefs, start + STEP * n, STEP)
                return 0

            lax.fori_loop(0, (stop - start) // STEP, step, 0)
            return 0

        lax.fori_loop(low, high, field, 0)

    def edges(g, p):
        def field(i, _):
            f = PF * p + i
            coefs = coefficients(g, f)
            block(g, f, coefs, 0, 2)
            block(g, f, coefs, CA - 2, 2)
            return 0

        lax.fori_loop(0, PF, field, 0)

    def fetch(i):
        return pltpu.make_async_copy(small[i][0], small[i][1], small_sem.at[i])

    for i in range(6):
        fetch(i).start()
    for i in range(len(LOADS)):
        load(i).start()
    barrier = pltpu.get_barrier_semaphore()

    def greet(r, s):
        pl.semaphore_signal(barrier, inc=1, device_id=(r, s), device_id_type=MESH)

    greet(row, after)
    greet(row, before)
    for d in range(1, 4):
        greet(row, x * 16 + ((y + d) % 4) * 4 + z)
        greet(row, x * 16 + y * 4 + (z + d) % 4)

    @pl.when(row <= 2)
    def _():
        greet(row + 1, sector)
        greet(row + 1, flipped)

    @pl.when(row >= 1)
    def _():
        greet(row - 1, sector)
        greet(row - 1, flipped)

    for i in range(6):
        fetch(i).wait()
    clear()
    pl.semaphore_wait(barrier, jnp.where(row == 0, 10, jnp.where(row == 3, 10, 12)))

    load(0).wait()
    load(1).wait()
    for p in range(PIECES):
        send_one(0, p)

    def send_halo(g, i):
        for up in range(2):
            halo(g, i, up).start()

    for n in range(5):
        load(2 + n).wait()
        if n < 2:
            send_halo(0, 2 * n)
            send_halo(0, 2 * n + 1)
    send_halo(0, N)
    send_halo(0, N + 1)

    for g in range(G):
        last = g == G - 1
        done, sent, steps = 0, 0, {"2": 0, "3": 0, "4": 0}
        for what in ORDER:
            if what == "C":
                wait_halo(g, done)
                interior(g, done)
                if last:
                    store(done).start()
                if g == 0 and done + 4 < N:
                    send_halo(0, done + 4)
                done += 1
            elif what == "H":
                if not last:
                    send_halo(g + 1, sent)
                sent += 1
            else:
                p = steps[what]
                steps[what] += 1
                if what == "2":
                    send_two(g, p)
                elif what == "3":
                    send_three(g, p)
                else:
                    if p == 0:
                        for i in (N, N + 1):
                            wait_halo(g, i)
                    ghosts(g, p)
                    edges(g, p)
                    if not last:
                        send_one(g + 1, p)
        for i in (N, N + 1):
            if last:
                store(i).start()
            else:
                send_halo(g + 1, i)

    arrived(result, store_sem)
    for g in range(G):
        arrived(q[g].at[:, 2 : CA + 2, 0:4, :], halo_send.at[g])
    for side in range(2):

        @pl.when(sends(side))
        def _():
            arrived(q[0].at[:, 0 : 2 * G, :, :], turn_send.at[0, side])

        @pl.when(active(side))
        def _():
            for n in range(1, 3):
                arrived(q[0].at[:, 0 : 3 * G, :, :], turn_send.at[n, side])


def on_device(state, interp_blocks, rotor_offset, axial_speed, row_swirl, diffusivity, coupling):
    def keep(value):
        return pltpu.with_memory_space_constraint(value, pltpu.HBM)

    interp_blocks, rotor_offset, coupling = keep(interp_blocks), keep(rotor_offset), keep(coupling)
    axial_speed, diffusivity = keep(axial_speed), keep(diffusivity)
    hbm = pl.BlockSpec(memory_space=pltpu.HBM)
    held = []
    for _ in range(2 * G * PIECES):
        for n in (2, 3, 4, 3, 4):
            held.append(pltpu.VMEM((n,) + PIECE, jnp.float32))
    dma = pltpu.SemaphoreType.DMA
    return pl.pallas_call(
        kernel,
        out_shape=jax.ShapeDtypeStruct(state.shape, jnp.float32),
        in_specs=[hbm] * 7,
        out_specs=pl.BlockSpec(memory_space=pl.ANY),
        scratch_shapes=[
            pltpu.VMEM(state.shape, jnp.float32),
            *[pltpu.VMEM((F, CA + 4, 32, CR), jnp.float32) for _ in range(G)],
            pltpu.VMEM(interp_blocks.shape, jnp.float32),
            pltpu.SMEM(rotor_offset.shape, jnp.int32),
            pltpu.SMEM(axial_speed.shape, jnp.float32),
            pltpu.SMEM(row_swirl.shape, jnp.float32),
            pltpu.SMEM(diffusivity.shape, jnp.float32),
            pltpu.SMEM(coupling.shape, jnp.float32),
            *held,
            dma((6,)),
            dma((len(LOADS),)),
            dma,
            dma((G,)),
            dma((G, N + 2)),
            dma((3, 2)),
            dma((3, G, 2, PIECES)),
        ],
        compiler_params=pltpu.CompilerParams(
            collective_id=0, has_side_effects=True, vmem_limit_bytes=48 * 1024 * 1024
        ),
    )(state, interp_blocks, rotor_offset, axial_speed, row_swirl, diffusivity, coupling)


def solution(mesh):
    return jax.shard_map(
        on_device,
        mesh=mesh,
        in_specs=(P(None, "row", "sector", None), P(), P(), P(), P("row"), P(), P()),
        out_specs=P(None, "row", "sector", None),
        check_vma=False,
    )
```

time: 130 us -> 104 us (0.80)
  Pallas kernels: 125 us -> 102 us
  local copies, waits for them, and re-layouts: 3.94 us -> 1.67 us
    pallas_call x1, Pallas kernels: 125 us -> 102 us  [on_device(): pl.pallas_call(kernel, out_shape=jax.ShapeDtypeStruct(state.shape, jnp.fl...]
    unnamed x1, local copies, waits for them, and re-layouts: 3.94 us -> 1.67 us
where the time goes in v2:
time: 104 us
  Pallas kernels  102 us (98%)
  local copies, waits for them, and re-layouts  1.67 us (2%)
    pallas_call x1, Pallas kernels, on_device(): pl.pallas_call(kernel, out_shape=jax.ShapeDtypeStruct(state.shape, jnp.fl...  102 us

profile of v2, /device:TPU:1, one launch (start us, length us, event | category | flops | bytes accessed | tf_op | source)
XLA Modules:
  0.0 104.1 jit_solution(2660947090730521926)
XLA Ops:
  0.7 101.8 %shard_map.73 = f32[6,64,16,128]{3,2,1,0:T(8,128)S(1)} custom-call(f32[6,64,16,128]{3,2,1,0:T(8,128)} %state.1, f32[16,16,32]{2,1,0:T(8,128)} %small_0.1, s32[4,3]{1,0:T(4,128)} %small_1.1, f32[6]{0:T(128)} %small_2.1, f32[1]{0:T(128)S(6)} %copy.9.small_3, f32[6]{0:T(128)} %small_4.1, f32[6,6]{1,0:T(8,128)} %small_5.1), custom_call_target="tpu_custom_call" | custom-call | tf_op jit(solution)/shard_map/pallas_call | solution.py:420
  102.4 1.7 %copy.10 = f32[6,64,16,128]{3,2,1,0:T(8,128)} copy(f32[6,64,16,128]{3,2,1,0:T(8,128)S(1)} %shard_map.73) | data formatting | bytes 6291456

commit v3 on v2

--- a/solution.py
+++ b/solution.py
@@ -15,12 +15,12 @@
 CR = 128
 G = 4
 LO = 8
-STEP = 4
+STEP = 12
 UNITS = tuple((2 + 12 * i, 14 + 12 * i, 3 * j, 3 * j + 3) for i in range(5) for j in range(2))
 CHUNKS = UNITS + ((0, 2, 0, 6), (62, 64, 0, 6))
 LOADS = ((0, 2), (62, 64)) + tuple((2 + 12 * i, 14 + 12 * i) for i in range(5))
 N = len(UNITS)
-ORDER = "CC2HC2HC2HC3HCHC3HCH3CHC4H4H4"
+ORDER = "CHCHC2HC2HC2HC3HC3HC3HCC4H4H4"
 PIECES = 3
 PF = F // PIECES
 PIECE = (PF, 2, CT, CR)
@@ -347,14 +347,15 @@
 
     for n in range(5):
         load(2 + n).wait()
-        if n < 2:
-            send_halo(0, 2 * n)
-            send_halo(0, 2 * n + 1)
+        for i in (2 * n, 2 * n + 1):
+            if i < N - ORDER.count("P"):
+                send_halo(0, i)
     send_halo(0, N)
     send_halo(0, N + 1)
 
     for g in range(G):
         last = g == G - 1
+        left = N - ORDER.count("P")
         done, sent, steps = 0, 0, {"2": 0, "3": 0, "4": 0}
         for what in ORDER:
             if what == "C":
@@ -362,9 +363,10 @@
                 interior(g, done)
                 if last:
                     store(done).start()
-                if g == 0 and done + 4 < N:
-                    send_halo(0, done + 4)
                 done += 1
+            elif what == "P":
+                send_halo(g, left)
+                left += 1
             elif what == "H":
                 if not last:
                     send_halo(g + 1, sent)

time: 104 us -> 102 us (0.981)
  Pallas kernels: 102 us -> 99.4 us
    pallas_call x1, Pallas kernels: 102 us -> 99.4 us  [on_device(): pl.pallas_call(kernel, out_shape=jax.ShapeDtypeStruct(state.shape, jnp.fl...]
where the time goes in v3:
time: 102 us
  Pallas kernels  99.4 us (97%)
  local copies, waits for them, and re-layouts  1.67 us (2%)
    pallas_call x1, Pallas kernels, on_device(): pl.pallas_call(kernel, out_shape=jax.ShapeDtypeStruct(state.shape, jnp.fl...  99.4 us

profile of v3, /device:TPU:1, one launch (start us, length us, event | category | flops | bytes accessed | tf_op | source)
XLA Modules:
  0.0 101.7 jit_solution(15527904108739273367)
XLA Ops:
  0.7 99.4 %shard_map.73 = f32[6,64,16,128]{3,2,1,0:T(8,128)S(1)} custom-call(f32[6,64,16,128]{3,2,1,0:T(8,128)} %state.1, f32[16,16,32]{2,1,0:T(8,128)} %small_0.1, s32[4,3]{1,0:T(4,128)} %small_1.1, f32[6]{0:T(128)} %small_2.1, f32[1]{0:T(128)S(6)} %copy.9.small_3, f32[6]{0:T(128)} %small_4.1, f32[6,6]{1,0:T(8,128)} %small_5.1), custom_call_target="tpu_custom_call" | custom-call | tf_op jit(solution)/shard_map/pallas_call | solution.py:422
  100.0 1.7 %copy.10 = f32[6,64,16,128]{3,2,1,0:T(8,128)} copy(f32[6,64,16,128]{3,2,1,0:T(8,128)S(1)} %shard_map.73) | data formatting | bytes 6291456

commit v4 on v3

--- a/solution.py
+++ b/solution.py
@@ -81,6 +81,14 @@
             result.at[f:e, a:b], out.at[f:e, a:b], store_sem
         )
 
+    def store_edges(p):
+        for a in (0, CA - 2):
+            pltpu.make_async_copy(
+                result.at[PF * p : PF * p + PF, a : a + 2],
+                out.at[PF * p : PF * p + PF, a : a + 2],
+                store_sem,
+            ).start()
+
     def halo(g, i, up):
         a, b, f, e = CHUNKS[i]
         source, target = (LO + CT - 2, LO - 2) if up else (LO, LO + CT)
@@ -147,7 +155,7 @@
                 arrived(held[g][side][p][0], turn_recv.at[0, g, side, p])
                 sx, sy, sz, _ = digits(g, side)
                 first, staged, second, _, _ = held[g][side][p]
-                for d in (1, 3, 2, 0):
+                for d in (2, 1, 3, 0):
                     target = (y + d) % 4
                     role = jnp.where(((target + sy) & 3) == y, 0, 1)
                     pick = (x + sx + ((target + sy + role) >> 2)) & 1
@@ -166,7 +174,7 @@
                 arrived(held[g][side][p][1], turn_recv.at[1, g, side, p])
                 sx, sy, sz, _ = digits(g, side)
                 _, _, second, staged, third = held[g][side][p]
-                for d in (1, 3, 2, 0):
+                for d in (2, 1, 3, 0):
                     target = (z + d) % 4
                     role = jnp.where(((target + sz) & 3) == z, 0, 1)
                     pick = (y + sy + ((target + sz + role) >> 2)) & 3
@@ -306,10 +314,6 @@
     def fetch(i):
         return pltpu.make_async_copy(small[i][0], small[i][1], small_sem.at[i])
 
-    for i in range(6):
-        fetch(i).start()
-    for i in range(len(LOADS)):
-        load(i).start()
     barrier = pltpu.get_barrier_semaphore()
 
     def greet(r, s):
@@ -331,6 +335,10 @@
         greet(row - 1, sector)
         greet(row - 1, flipped)
 
+    for i in range(6):
+        fetch(i).start()
+    for i in range(len(LOADS)):
+        load(i).start()
     for i in range(6):
         fetch(i).wait()
     clear()
@@ -384,12 +392,12 @@
                             wait_halo(g, i)
                     ghosts(g, p)
                     edges(g, p)
-                    if not last:
+                    if last:
+                        store_edges(p)
+                    else:
                         send_one(g + 1, p)
-        for i in (N, N + 1):
-            if last:
-                store(i).start()
-            else:
+        if not last:
+            for i in (N, N + 1):
                 send_halo(g + 1, i)
 
     arrived(result, store_sem)

time: 102 us -> 101 us (level)
  no operation moved by 1% of the time
where the time goes in v4:
time: 101 us
  Pallas kernels  98.6 us (98%)
  local copies, waits for them, and re-layouts  1.67 us (2%)
    pallas_call x1, Pallas kernels, on_device(): pl.pallas_call(kernel, out_shape=jax.ShapeDtypeStruct(state.shape, jnp.fl...  98.6 us

profile of v4, /device:TPU:1, one launch (start us, length us, event | category | flops | bytes accessed | tf_op | source)
XLA Modules:
  0.0 100.9 jit_solution(11444787422840998379)
XLA Ops:
  0.7 98.6 %shard_map.73 = f32[6,64,16,128]{3,2,1,0:T(8,128)S(1)} custom-call(f32[6,64,16,128]{3,2,1,0:T(8,128)} %state.1, f32[16,16,32]{2,1,0:T(8,128)} %small_0.1, s32[4,3]{1,0:T(4,128)} %small_1.1, f32[6]{0:T(128)} %small_2.1, f32[1]{0:T(128)S(6)} %copy.9.small_3, f32[6]{0:T(128)} %small_4.1, f32[6,6]{1,0:T(8,128)} %small_5.1), custom_call_target="tpu_custom_call" | custom-call | tf_op jit(solution)/shard_map/pallas_call | solution.py:430
  99.3 1.7 %copy.10 = f32[6,64,16,128]{3,2,1,0:T(8,128)} copy(f32[6,64,16,128]{3,2,1,0:T(8,128)S(1)} %shard_map.73) | data formatting | bytes 6291456
